TPU v7x, 32 devices: a whole 2x2x4 slice. The times are simulated.
32 devices in a mesh: seq: 8 (over z, x), tier: 4 (over y, core).
Axes of the slice: x: 2, y: 2, z: 4, core: 2. Of those that a mesh axis runs over, the one named last changes fastest.
Arguments:
- layer_input: bfloat16 [8, 512, 1024], P('seq', 'tier'), may hold values from -6 to 6
- memory: bfloat16 [8, 512, 1024], P('seq', 'tier'), may hold values from -6 to 6
- compressed: bfloat16 [8, 512, 1024], P('seq', 'tier'), may hold values from -6 to 6
- seg_len: int32 [8], P('seq'), may hold values from 1 to 512, as said below
- hist_len: int32 [8], P('seq'), may hold values from 0 to 1024, as said below
- query_weight: bfloat16 [1024, 1024], replicated, may hold values from -0.1875 to 0.1875
- key_weight: bfloat16 [1024, 1024], replicated, may hold values from -0.1875 to 0.1875
- value_weight: bfloat16 [1024, 1024], replicated, may hold values from -0.1875 to 0.1875
- attn_out_weight: bfloat16 [1024, 1024], replicated, may hold values from -1 to 1
- ffn_in_weight: bfloat16 [1024, 4096], replicated, may hold values from -0.1875 to 0.1875
- ffn_out_weight: bfloat16 [4096, 1024], replicated, may hold values from -0.09375 to 0.09375
- norm_gain: float32 [1024], replicated, may hold values from 0.1 to 1.9
- head_slope: float32 [8], replicated, may hold values from 0.0005 to 0.05
- comp_weight: bfloat16 [3072, 1024], replicated, may hold values from -0.109375 to 0.109375
- cotangent: bfloat16 [8, 512, 1024], P('seq', 'tier'), may hold values from -6 to 6
Outputs:
- output: bfloat16 [8, 512, 1024], P('seq', 'tier')
- grad_input: float32 [8, 512, 1024], P('seq', 'tier')
- new_memory: bfloat16 [8, 512, 1024], P('seq', 'tier')
- new_compressed: bfloat16 [8, 512, 1024], P('seq', 'tier')
- grad_query_weight: float32 [1024, 1024], P('seq', 'tier')
- grad_key_weight: float32 [1024, 1024], P('seq', 'tier')
- grad_value_weight: float32 [1024, 1024], P('seq', 'tier')
- grad_attn_out_weight: float32 [1024, 1024], P('seq', 'tier')
- grad_ffn_in_weight: float32 [1024, 4096], P('seq', 'tier')
- grad_ffn_out_weight: float32 [4096, 1024], P('seq', 'tier')
- grad_comp_weight: float32 [3072, 1024], P('seq', 'tier')
- grad_norm_gain: float32 [1024], replicated
- grad_head_slope: float32 [8], replicated
Inputs may be any that keep to these rules, and one draw needn't show every extreme that they name: `seg_len`: the first sequence's segment is full; others may end early, as the last segment of a book does. `hist_len`: the first sequence has a full history; a book's early segments have a short one.
All inputs are finite; a program needn't handle non-finite values.
Results may differ from a plain program's by a relative error of at most 0.014.
Values may be sent and summed in bfloat16 or wider, within the bound.
A program may use at most 256 MiB of HBM per device.

v0:
```python
import math
import jax
import jax.numpy as jnp
from jax import lax
from jax.sharding import PartitionSpec as P

norm_eps = 1e-05
neg_large = -1e30
f32 = jnp.float32
bf16 = jnp.bfloat16


def gelu_tanh(values_in):
    return jax.nn.gelu(values_in, approximate=True)


def layer_norm(residual, norm_gain):
    centre = jnp.mean(residual, axis=-1, keepdims=True)
    deviation = residual - centre
    variance = jnp.mean(deviation * deviation, axis=-1, keepdims=True)
    return deviation * lax.rsqrt(variance + norm_eps) * norm_gain


def softmax_grad(weights, grad_weights):
    inner_sum = jnp.sum(weights * grad_weights, axis=-1, keepdims=True)
    return (weights * (grad_weights - inner_sum)).astype(bf16)


def mm(left, right):
    return jnp.dot(left, right, preferred_element_type=f32)


def mm_tn(left, right):
    return lax.dot_general(left, right, (((0,), (0,)), ((), ())), preferred_element_type=f32)


def mm_nt(left, right):
    return lax.dot_general(left, right, (((1,), (1,)), ((), ())), preferred_element_type=f32)


def per_device(
    layer_input,
    memory,
    compressed,
    seg_len,
    hist_len,
    query_weight,
    key_weight,
    value_weight,
    attn_out_weight,
    ffn_in_weight,
    ffn_out_weight,
    norm_gain,
    head_slope,
    comp_weight,
    cotangent,
):
    _, row_count, width = layer_input.shape
    tiers = lax.axis_size("tier")
    seqs = lax.axis_size("seq")
    tier_pos = lax.axis_index("tier")
    heads = head_slope.shape[0]
    head_dim = width // heads
    hpt = heads // tiers
    cb = hpt * head_dim
    ff = ffn_in_weight.shape[1]
    ffb = ff // tiers
    seg = row_count * tiers
    keys_n = 3 * seg
    ncomp = (seg + 2) // 3
    inv_root = 1.0 / math.sqrt(head_dim)
    length = seg_len[0]
    history = hist_len[0]
    own_ids = tier_pos * row_count + jnp.arange(row_count, dtype=jnp.int32)
    mask_own = (own_ids < length).astype(f32)[:, None]
    all_ids = jnp.arange(seg, dtype=jnp.int32)
    mask_all = (all_ids < length).astype(f32)[:, None]
    hidden_own = (layer_input[0].astype(f32) * mask_own).astype(bf16)
    raw_local = jnp.stack([compressed[0], memory[0], hidden_own], axis=0)
    raw_seq = lax.all_gather(raw_local, "tier", axis=1, tiled=True)
    cot_seq = lax.all_gather(cotangent[0], "tier", axis=0, tiled=True)
    context = raw_seq.reshape(keys_n, width)
    comp_rows = raw_seq[0]
    memory_rows = raw_seq[1]
    hidden_seq = raw_seq[2]
    col0 = tier_pos * cb
    wq_t = lax.dynamic_slice_in_dim(query_weight, col0, cb, axis=1)
    wk_t = lax.dynamic_slice_in_dim(key_weight, col0, cb, axis=1)
    wv_t = lax.dynamic_slice_in_dim(value_weight, col0, cb, axis=1)
    wkv_t = jnp.concatenate([wk_t, wv_t], axis=1)
    slope_t = lax.dynamic_slice_in_dim(head_slope, tier_pos * hpt, hpt)
    q_t = mm(hidden_seq, wq_t).astype(bf16)
    kv_t = mm(context, wkv_t).astype(bf16)
    q_h = q_t.reshape(seg, hpt, head_dim)
    k_h = kv_t[:, :cb].reshape(keys_n, hpt, head_dim)
    v_h = kv_t[:, cb:].reshape(keys_n, hpt, head_dim)
    key_ids = jnp.arange(keys_n, dtype=jnp.int32)
    offsets = (2 * seg + all_ids)[:, None] - key_ids[None, :]
    distance = offsets.astype(f32)
    in_history = (key_ids[None, :] < 2 * seg) & (key_ids[None, :] >= 2 * seg - history)
    in_segment = (key_ids[None, :] >= 2 * seg) & (offsets >= 0)
    key_valid = (in_history | in_segment)[None]
    scores = jnp.einsum("rhd,khd->hrk", q_h, k_h, preferred_element_type=f32) * inv_root
    scores = scores - slope_t[:, None, None] * distance[None]
    masked = jnp.where(key_valid, scores, neg_large)
    log_total = jax.nn.logsumexp(masked, axis=-1, keepdims=True)
    probs = jnp.exp(masked - log_total)
    probs_low = probs.astype(bf16)
    attended_t = jnp.einsum("hrk,khd->rhd", probs_low, v_h, preferred_element_type=f32)
    attended_t = attended_t.reshape(seg, cb).astype(bf16)
    attended = lax.all_to_all(attended_t, "tier", 0, 1, tiled=True)
    mem_k = k_h[seg : 2 * seg]
    mem_v = v_h[seg : 2 * seg]
    mem_scores = jnp.einsum("rhd,khd->hrk", q_h, mem_k, preferred_element_type=f32) * inv_root
    mem_probs = jax.nn.softmax(mem_scores, axis=-1).astype(bf16)
    from_memory = jnp.einsum("hrk,khd->rhd", mem_probs, mem_v, preferred_element_type=f32)
    padded = jnp.pad(memory_rows, ((0, 3 * ncomp - seg), (0, 0)))
    windows = padded.reshape(ncomp, 3 * width)
    comp_new = mm(windows, comp_weight).astype(bf16)
    ckv_t = mm(comp_new, wkv_t).astype(bf16)
    comp_k = ckv_t[:, :cb].reshape(ncomp, hpt, head_dim)
    comp_v = ckv_t[:, cb:].reshape(ncomp, hpt, head_dim)
    comp_scores = jnp.einsum("rhd,khd->hrk", q_h, comp_k, preferred_element_type=f32) * inv_root
    comp_probs = jax.nn.softmax(comp_scores, axis=-1)
    comp_low = comp_probs.astype(bf16)
    from_comp = jnp.einsum("hrk,khd->rhd", comp_low, comp_v, preferred_element_type=f32)
    grad_fc = ((from_comp - from_memory) * mask_all[:, :, None]).astype(bf16)
    grad_cw = jnp.einsum("rhd,khd->hrk", grad_fc, comp_v, preferred_element_type=f32)
    grad_cs = softmax_grad(comp_probs, grad_cw)
    grad_ck = (
        jnp.einsum("hrk,rhd->khd", grad_cs, q_h, preferred_element_type=f32) * inv_root
    ).astype(bf16)
    grad_cv = jnp.einsum("hrk,rhd->khd", comp_low, grad_fc, preferred_element_type=f32).astype(bf16)
    grad_ckv = jnp.concatenate([grad_ck.reshape(ncomp, cb), grad_cv.reshape(ncomp, cb)], axis=1)
    grad_comp_part = mm_nt(grad_ckv, wkv_t)
    grad_comp_t = lax.psum_scatter(grad_comp_part, "tier", scatter_dimension=1, tiled=True)
    grad_comp_t = grad_comp_t.astype(bf16)
    part_comp = mm_tn(windows, grad_comp_t)
    full_comp = jnp.concatenate([comp_rows[ncomp:], comp_new[:ncomp]], axis=0)
    new_compressed = lax.dynamic_slice_in_dim(full_comp, tier_pos * row_count, row_count, axis=0)
    hidden_f = hidden_own.astype(f32)
    residual = hidden_f + mm(attended, attn_out_weight)
    normed, norm_pull = jax.vjp(layer_norm, residual, norm_gain)
    normed_low = normed.astype(bf16)
    pre_act = mm(normed_low, ffn_in_weight)
    act_value, gelu_pull = jax.vjp(gelu_tanh, pre_act)
    activation = act_value.astype(bf16)
    ffn_result = mm(activation, ffn_out_weight)
    output = ((residual + ffn_result) * mask_own).astype(bf16)
    grad_rows = cotangent[0].astype(f32) * mask_own
    grad_low = grad_rows.astype(bf16)
    grad_act = mm_nt(grad_low, ffn_out_weight)
    grad_pre = gelu_pull(grad_act)[0].astype(bf16)
    grad_normed = mm_nt(grad_pre, ffn_in_weight)
    grad_resid_norm, part_gain = norm_pull(grad_normed)
    grad_resid = grad_rows + grad_resid_norm
    grad_att = grad_resid.astype(bf16)
    grad_attended = mm_nt(grad_att, attn_out_weight).astype(bf16)
    back_t = lax.all_to_all(jnp.stack([grad_attended, grad_att], axis=0), "tier", 2, 1, tiled=True)
    grad_attended_t = back_t[0]
    grad_att_t = back_t[1]
    fwd_seq = lax.all_gather(jnp.stack([normed_low, attended], axis=0), "tier", axis=1, tiled=True)
    normed_seq = fwd_seq[0]
    attended_seq = fwd_seq[1]
    grad_seq = (cot_seq.astype(f32) * mask_all).astype(bf16)
    pre_seq = mm(normed_seq, ffn_in_weight)
    act_seq = gelu_tanh(pre_seq).astype(bf16)
    fcol0 = tier_pos * ffb
    pre_seq_t = lax.dynamic_slice_in_dim(pre_seq, fcol0, ffb, axis=1)
    wfo_t = lax.dynamic_slice_in_dim(ffn_out_weight, fcol0, ffb, axis=0)
    grad_act_seq_t = mm_nt(grad_seq, wfo_t)
    _, gelu_pull_seq = jax.vjp(gelu_tanh, pre_seq_t)
    grad_pre_seq_t = gelu_pull_seq(grad_act_seq_t)[0].astype(bf16)
    grad_seq_t = lax.dynamic_slice_in_dim(grad_seq, col0, cb, axis=1)
    part_ffn_in = mm_tn(normed_seq, grad_pre_seq_t)
    part_ffn_out = mm_tn(act_seq, grad_seq_t)
    part_attn_out = mm_tn(attended_seq, grad_att_t)
    grad_att_h = grad_attended_t.reshape(seg, hpt, head_dim)
    grad_probs = jnp.einsum("rhd,khd->hrk", grad_att_h, v_h, preferred_element_type=f32)
    grad_scores = softmax_grad(probs, grad_probs)
    part_slope = -jnp.einsum("hrk,rk->h", grad_scores.astype(f32), distance)
    grad_q = (
        (jnp.einsum("hrk,khd->rhd", grad_scores, k_h, preferred_element_type=f32) * inv_root)
        .reshape(seg, cb)
        .astype(bf16)
    )
    grad_k = (
        (jnp.einsum("hrk,rhd->khd", grad_scores, q_h, preferred_element_type=f32) * inv_root)
        .reshape(keys_n, cb)
        .astype(bf16)
    )
    grad_v = jnp.einsum("hrk,rhd->khd", probs_low, grad_att_h, preferred_element_type=f32)
    grad_v = grad_v.reshape(keys_n, cb).astype(bf16)
    part_query = mm_tn(hidden_seq, grad_q)
    part_key = mm_tn(context, grad_k)
    part_value = mm_tn(context, grad_v)
    seg_grads = jnp.stack([grad_q, grad_k[2 * seg :], grad_v[2 * seg :]], axis=0)
    own_grads = lax.all_to_all(seg_grads, "tier", 1, 2, tiled=True)
    grad_hidden = grad_resid + mm_nt(own_grads[0], query_weight)
    grad_hidden = grad_hidden + mm_nt(own_grads[1], key_weight)
    grad_hidden = grad_hidden + mm_nt(own_grads[2], value_weight)
    grad_input = grad_hidden * mask_own
    parts = (part_query, part_key, part_value, part_attn_out, part_ffn_in, part_ffn_out, part_comp)
    flat = jnp.concatenate([p.reshape(seqs, -1, width) for p in parts], axis=1)
    flat = flat.reshape(-1, width)
    reduced = lax.psum_scatter(flat, "seq", scatter_dimension=0, tiled=True).reshape(-1)
    outs = []
    start = 0
    for p in parts:
        size = p.size // seqs
        outs.append(reduced[start : start + size].reshape(p.shape[0] // seqs, p.shape[1]))
        start += size
    slope_full = lax.dynamic_update_slice_in_dim(
        jnp.zeros((heads,), f32), part_slope, tier_pos * hpt, 0
    )
    gain_total, slope_total = lax.psum((part_gain, slope_full), ("seq", "tier"))
    return (
        output[None],
        grad_input[None],
        hidden_own[None],
        new_compressed[None],
        outs[0],
        outs[1],
        outs[2],
        outs[3],
        outs[4],
        outs[5],
        outs[6],
        gain_total,
        slope_total,
    )


def solution(mesh):
    placed = (
        P("seq", "tier", None),
        P("seq", "tier", None),
        P("seq", "tier", None),
        P("seq"),
        P("seq"),
        P(),
        P(),
        P(),
        P(),
        P(),
        P(),
        P(),
        P(),
        P(),
        P("seq", "tier", None),
    )
    return jax.shard_map(
        per_device,
        mesh=mesh,
        in_specs=placed,
        out_specs=(
            P("seq", "tier", None),
            P("seq", "tier", None),
            P("seq", "tier", None),
            P("seq", "tier", None),
            P("seq", "tier"),
            P("seq", "tier"),
            P("seq", "tier"),
            P("seq", "tier"),
            P("seq", "tier"),
            P("seq", "tier"),
            P("seq", "tier"),
            P(),
            P(),
        ),
        check_vma=False,
    )
```

profile of v0, /device:TPU:0, one launch (start us, length us, event | category | flops | bytes accessed | tf_op | source)
XLA Modules:
  0.0 487.0 jit_solution(13463608105993968197)
XLA Ops:
  12.6 3.1 fusion.52
  19.5 23.7 %all-gather.5.cloned.1.call-done = bf16[3,512,1024]{2,1,0:T(8,128)(2,1)} async-done(((bf16[3,128,1024]{2,1,0:T(8,128)(2,1)}), bf16[3,512,1024]{2,1,0:T(8,128)(2,1)}) %all-gather.5.cloned.1.call-update) | async-done | bytes 3145744 | tf_op jit(solution)/shard_map/all_gather | solution.py:80
  43.2 3.7 convolution_convert_fusion
  47.1 2.8 convolution_convert_fusion.5
  57.4 3.4 all-to-all-start
  63.2 2.9 reshape.323
  66.1 4.5 convolution_convert_fusion.2
  82.4 3.1 fusion.54
  92.8 2.6 fusion.93
  98.0 6.0 %fusion.167 = f32[128,4096]{1,0:T(8,128)} fusion(bf16[1024,4096]{1,0:T(8,128)(2,1)} %param.24, f32[128,1024]{1,0:T(8,128)S(1)} %get-tuple-element.44, f32[1024]{0:T(1024)S(1)} %copy-done.38, f32[128]{0:T(128)S(1)} %fusion.135, f32[128]{0:T(128)S(1)} %broadcast_multiply_fusion), kind=kOutput, calls=%fused_computation.219 | convolution fusion | flops 1074266112 | bytes 11015168 | tf_op jit(solution)/shard_map/dot_general | solution.py:30
  104.0 13.6 %multiply_reduce_fusion.4 = (f32[1024]{0:T(1024)S(1)}, f32[128]{0:T(128)S(1)}, f32[128,1024]{1,0:T(8,128)}) fusion(f32[128,1024]{1,0:T(8,128)S(1)} %get-tuple-element.44, f32[128]{0:T(128)S(1)} %fusion.135, f32[128]{0:T(128)S(1)} %broadcast_multiply_fusion, f32[1024]{0:T(1024)S(1)} %copy-done.38, bf16[1024,4096]{1,0:T(8,128)(2,1)} %param.24, ...), kind=kOutput, calls=%fused_computation.135 | convolution fusion | flops 2159279104 | bytes 20195328 | tf_op jit(solution)/shard_map/dot_general | solution.py:38
  123.5 3.5 all-to-all-start.1
  127.1 2.5 fusion.32
  130.7 5.1 %all-to-all-done.1 = bf16[2,128,1024]{1,0,2:T(2,128)(2,1)S(1)} async-done(((bf16[2,128,1024]{1,0,2:T(2,128)(2,1)}), bf16[2,128,1024]{1,0,2:T(2,128)(2,1)S(1)}, u32[]{:S(2)}, u32[]{:S(2)}) %all-to-all-start.1) | async-done | bytes 524320 | tf_op jit(solution)/shard_map/all_to_all | solution.py:159
  137.0 4.9 %multiply_reduce_fusion.1 = (f32[2,512]{1,0:T(2,128)S(1)}, f32[2,512,1536]{2,1,0:T(8,128)S(1)}) fusion(f32[2,512,1536]{2,1,0:T(8,128)} %copy-done.2, f32[2,512]{1,0:T(2,128)S(1)} %log_add_fusion, bf16[512,2,128]{0,2,1:T(8,128)(2,1)S(1)} %reshape.348, bf16[1536,2,128]{0,2,1:T(8,128)(2,1)S(1)} %bitcast.169), kind=kOutput, calls=%fused_computation.13 | convolution fusion | flops 407370752 | bytes 13639680 | tf_op jit(solution)/shard_map/rhd,khd->hrk/dot_general | solution.py:179
  141.9 4.7 multiply_reduce_fusion
  152.6 2.6 fusion.17
  157.8 4.2 convolution_convert_fusion.1
  171.1 3.2 fusion.117
  174.3 4.8 reshape.333
  183.8 7.3 %fusion.63 = f32[512,4096]{1,0:T(8,128)S(1)} fusion(bf16[1024,4096]{1,0:T(8,128)(2,1)} %param.24, bf16[2,512,1024]{2,1,0:T(8,128)(2,1)} %all-gather.7.cloned.1.call-done), kind=kOutput, calls=%fused_computation.98 | convolution fusion | flops 4294967296 | bytes 17825792 | tf_op jit(solution)/shard_map/dot_general | solution.py:30
  191.1 3.3 copy-done.41
  194.4 4.8 fusion.11
  199.2 5.2 %reshape.328 = f32[8,128,1024]{2,1,0:T(8,128)} reshape(f32[4096,256]{1,0:T(8,128)} %fusion.11) | data formatting | bytes 8388608 | tf_op jit(solution)/shard_map/reshape | solution.py:204
  205.5 7.7 %convolution_dynamic-update-slice_fusion = f32[8,480,1024]{2,1,0:T(8,128)} fusion(f32[8,480,1024]{2,1,0:T(8,128)} %constant_dynamic-update-slice_fusion.2, bf16[8,128,512]{2,1,0:T(8,128)(2,1)} %bitcast.187, f32[512,4096]{1,0:T(8,128)} %copy-done.41, s32[]{:T(128)S(6)} %select_n.37, bf16[512,1024]{1,0:T(8,128)(2,1)S(1)} %copy-done.24, ...), kind=kOutput, calls=%fused_computation.30 | convolution fusion | flops 2157969408 | bytes 10486784 | tf_op jit(solution)/shard_map/dot_general | solution.py:34
  213.2 4.9 %constant_dynamic-update-slice_fusion.1 = f32[8,480,1024]{2,1,0:T(8,128)} fusion(f32[8,480,1024]{2,1,0:T(8,128)} %convolution_dynamic-update-slice_fusion, f32[8,128,1024]{2,1,0:T(8,128)} %reshape.328), kind=kLoop, calls=%fused_computation.164 | loop fusion | bytes 8388608
  224.7 2.8 pad_maximum_fusion.1
  227.5 3.5 all-to-all-start.2
  231.0 6.3 %fusion.56 = bf16[1,128,1024]{2,1,0:T(8,128)(2,1)} fusion(f32[128,1024]{1,0:T(8,128)S(1)} %get-tuple-element.44, bf16[4096,1024]{1,0:T(8,128)(2,1)} %param.25, f32[128,4096]{1,0:T(8,128)} %fusion.167, f32[128]{0:T(128)S(1)} %compare_convert_fusion), kind=kOutput, calls=%fused_computation.83 | convolution fusion | flops 1078853632 | bytes 11272704 | tf_op jit(solution)/shard_map/dot_general | solution.py:30
  237.4 47.4 %all-reduce.1 = (f32[1024]{0:T(1024)}, f32[8]{0:T(128)}) all-reduce(f32[1024]{0:T(1024)S(1)} %get-tuple-element.13, f32[8]{0:T(128)S(1)} %negate_dynamic-update-slice_fusion), channel_id=1, replica_groups=mesh['seq'=8,'tier'=4] {'seq','tier'}, use_global_device_ids=true, to_apply=%region_15.16 | all-reduce | flops 1032 | bytes 8256 | tf_op jit(solution)/shard_map/psum | solution.py:216
  285.5 2.9 convolution_add_fusion.2
  292.5 179.6 %reduce-scatter.5.cloned.1.call-done = f32[480,1024]{1,0:T(8,128)} async-done(((f32[3840,1024]{1,0:T(8,128)}), f32[480,1024]{1,0:T(8,128)}) %reduce-scatter.5.cloned.1.call-update) | async-done | bytes 1966096 | tf_op jit(solution)/shard_map/reduce_scatter | solution.py:206
  (194 shorter events, 90.0 us)
Async XLA Ops:
  7.2 89.0 %copy-start = (bf16[1024,1024]{1,0:T(8,128)(2,1)S(1)}, bf16[1024,1024]{1,0:T(8,128)(2,1)}, u32[]{:S(2)}) copy-start(bf16[1024,1024]{1,0:T(8,128)(2,1)} %param.23) | copy-start | bytes 6291460
  7.2 36.0 %all-gather.5.cloned.1.call-start = ((), (), s32[]{:S(2)}) async-start(), calls=%async_computation.5 | async-start | bytes 3932160 | tf_op jit(solution)/shard_map/all_gather | solution.py:80
  11.8 115.3 %all-gather.9.cloned.1.call-start = ((), (), s32[]{:S(2)}) async-start(), calls=%async_computation.9 | async-start | bytes 1310720 | tf_op jit(solution)/shard_map/all_gather | solution.py:81
  19.5 23.7 %copy-start.33 = (bf16[1024,256]{1,0:T(8,128)(2,1)}, bf16[1024,256]{1,0:T(8,128)(2,1)S(1)}, u32[]{:S(2)}) copy-start(bf16[1024,256]{1,0:T(8,128)(2,1)S(1)} %get-tuple-element.53) | copy-start | bytes 1572868
  19.5 27.4 %copy-start.31 = (bf16[1024,256]{1,0:T(8,128)(2,1)}, bf16[1024,256]{1,0:T(8,128)(2,1)S(1)}, u32[]{:S(2)}) copy-start(bf16[1024,256]{1,0:T(8,128)(2,1)S(1)} %get-tuple-element.52) | copy-start | bytes 1572868
  47.1 6.6 %copy-start.7 = (bf16[1536,256]{0,1:T(8,128)(2,1)}, bf16[1536,256]{0,1:T(8,128)(2,1)S(1)}, u32[]{:S(2)}) copy-start(bf16[1536,256]{0,1:T(8,128)(2,1)S(1)} %get-tuple-element.30) | copy-start | bytes 2359300
  57.4 38.1 %all-to-all-start = ((bf16[4,128,256]{1,2,0:T(8,128)(2,1)}), bf16[4,128,256]{1,2,0:T(8,128)(2,1)S(1)}, u32[]{:S(2)}, u32[]{:S(2)}) async-start(bf16[4,128,256]{1,2,0:T(8,128)(2,1)} %copy.122), calls=%async_computation | async-start | bytes 524288 | tf_op jit(solution)/shard_map/all_to_all | solution.py:111
  60.8 110.3 %reduce-scatter.3.cloned.1.call-start = ((), (), s32[]{:S(2)}) async-start(), calls=%async_computation.7 | async-start | bytes 901120 | tf_op jit(solution)/shard_map/reduce_scatter | solution.py:136
  66.1 4.5 copy-start.32
  66.1 4.5 copy-start.34
  66.1 7.5 %copy-start.29 = (bf16[512,256]{0,1:T(8,128)(2,1)S(1)}, bf16[512,256]{0,1:T(8,128)(2,1)}, u32[]{:S(2)}) copy-start(bf16[512,256]{0,1:T(8,128)(2,1)} %copy-done.28) | copy-start | bytes 786436
  92.8 5.1 %copy-start.38 = (f32[1024]{0:T(1024)S(1)}, f32[1024]{0:T(1024)}, u32[]{:S(2)}) copy-start(f32[1024]{0:T(1024)} %param.26) | copy-start | bytes 12292
  122.4 7.3 %copy-start.21 = (bf16[4,128,256]{1,2,0:T(8,128)(2,1)S(1)}, bf16[4,128,256]{1,2,0:T(8,128)(2,1)}, u32[]{:S(2)}) copy-start(bf16[4,128,256]{1,2,0:T(8,128)(2,1)} %copy-done.20) | copy-start | bytes 786436
  122.4 7.4 %copy-start.27 = (bf16[1,128,1024]{2,1,0:T(8,128)(2,1)S(1)}, bf16[1,128,1024]{2,1,0:T(8,128)(2,1)}, u32[]{:S(2)}) copy-start(bf16[1,128,1024]{2,1,0:T(8,128)(2,1)} %get-tuple-element.34) | copy-start | bytes 786436
  123.5 12.3 %all-to-all-start.1 = ((bf16[2,128,1024]{1,0,2:T(2,128)(2,1)}), bf16[2,128,1024]{1,0,2:T(2,128)(2,1)S(1)}, u32[]{:S(2)}, u32[]{:S(2)}) async-start(bf16[2,128,1024]{1,0,2:T(2,128)(2,1)} %copy.123), calls=%async_computation.1 | async-start | bytes 1048576 | tf_op jit(solution)/shard_map/all_to_all | solution.py:159
  127.0 52.1 %all-gather.7.cloned.1.call-start = ((), (), s32[]{:S(2)}) async-start(), calls=%async_computation.6 | async-start | bytes 2621440 | tf_op jit(solution)/shard_map/all_gather | solution.py:162
  129.6 7.4 %copy-start.8 = (bf16[1536,256]{0,1:T(8,128)(2,1)S(1)}, bf16[1536,256]{0,1:T(8,128)(2,1)}, u32[]{:S(2)}) copy-start(bf16[1536,256]{0,1:T(8,128)(2,1)} %copy-done.7) | copy-start | bytes 2359300
  130.6 341.4 %reduce-scatter.5.cloned.1.call-start = ((), (), s32[]{:S(2)}) async-start(), calls=%async_computation.8 | async-start | bytes 17694720 | tf_op jit(solution)/shard_map/reduce_scatter | solution.py:206
  137.0 4.9 %copy-start.4 = (f32[1536,512]{0,1:T(8,128)S(1)}, f32[1536,512]{0,1:T(8,128)}, u32[]{:S(2)}) copy-start(f32[1536,512]{0,1:T(8,128)} %get-tuple-element.39) | copy-start | bytes 9437188
  149.4 5.8 %copy-start.18 = (bf16[2,128,512]{2,1,0:T(8,128)(2,1)}, bf16[2,128,512]{2,1,0:T(8,128)(2,1)S(1)}, u32[]{:S(2)}) copy-start(bf16[2,128,512]{2,1,0:T(8,128)(2,1)S(1)} %fusion.50) | copy-start | bytes 786436
  165.2 4.8 copy-start.12
  165.2 5.9 %copy-start.11 = (bf16[171,3072]{1,0:T(8,128)(2,1)S(1)}, bf16[171,3072]{1,0:T(8,128)(2,1)}, u32[]{:S(2)}) copy-start(bf16[171,3072]{1,0:T(8,128)(2,1)} %reshape.323) | copy-start | bytes 3151876
  174.3 4.9 copy-start.37
  183.8 10.6 %copy-start.24 = (bf16[512,1024]{1,0:T(8,128)(2,1)S(1)}, bf16[512,1024]{1,0:T(8,128)(2,1)}, u32[]{:S(2)}) copy-start(bf16[512,1024]{1,0:T(8,128)(2,1)} %fusion.32) | copy-start | bytes 3145732
  213.2 4.9 %copy-start.5 = (f32[8,96,1024]{2,1,0:T(8,128)S(1)}, f32[8,96,1024]{2,1,0:T(8,128)}, u32[]{:S(2)}) copy-start(f32[8,96,1024]{2,1,0:T(8,128)} %reshape.333) | copy-start | bytes 9437188
  219.9 4.3 copy-start.19
  227.5 57.3 %all-to-all-start.2 = ((bf16[3,512,256]{2,0,1:T(4,128)(2,1)}), bf16[3,512,256]{2,0,1:T(4,128)(2,1)S(1)}, u32[]{:S(2)}, u32[]{:S(2)}) async-start(bf16[3,512,256]{2,0,1:T(4,128)(2,1)} %pad_maximum_fusion.1), calls=%async_computation.2 | async-start | bytes 2097152 | tf_op jit(solution)/shard_map/all_to_all | solution.py:198
  237.3 48.2 %copy-start.10 = (f32[128,1024]{1,0:T(8,128)S(1)}, f32[128,1024]{1,0:T(8,128)}, u32[]{:S(2)}) copy-start(f32[128,1024]{1,0:T(8,128)} %copy-done.9) | copy-start | bytes 1572868
  237.3 48.2 %copy-start.22 = (bf16[1,128,1024]{2,1,0:T(8,128)(2,1)S(1)}, bf16[1,128,1024]{2,1,0:T(8,128)(2,1)}, u32[]{:S(2)}) copy-start(bf16[1,128,1024]{2,1,0:T(8,128)(2,1)} %param.29) | copy-start | bytes 786436
  285.5 5.3 %copy-start.13 = (bf16[1024,1024]{1,0:T(8,128)(2,1)S(1)}, bf16[1024,1024]{1,0:T(8,128)(2,1)}, u32[]{:S(2)}) copy-start(bf16[1024,1024]{1,0:T(8,128)(2,1)} %param.22) | copy-start | bytes 6291460
  472.1 7.1 %slice-start = ((f32[480,1024]{1,0:T(8,128)}), f32[96,1024]{1,0:T(8,128)S(1)}, s32[]{:S(2)}) async-start(f32[480,1024]{1,0:T(8,128)} %reduce-scatter.5.cloned.1.call-done), calls=%async_computation.10 | async-start | bytes 786432 | tf_op jit(solution)/shard_map/slice | solution.py:211
  472.1 7.9 %copy-start.1 = (bf16[1024,1024]{1,0:T(8,128)(2,1)S(1)}, bf16[1024,1024]{1,0:T(8,128)(2,1)}, u32[]{:S(2)}) copy-start(bf16[1024,1024]{1,0:T(8,128)(2,1)} %param.23) | copy-start | bytes 6291460
  (19 other events, 46.1 us)
Sparse Core Ops, SparseCore 0:
  12.0 31.2 all-gather.4
  44.8 16.7 all-gather.8
  95.6 24.2 reduce-scatter.2
  130.8 23.9 all-gather.6
  220.1 251.9 reduce-scatter.4
where the time goes:
time: 495 us; the launch traced here: 487 us
  waiting for transfers between devices  209 us (42%)
  matrix products  110 us (22%)
  local copies, waits for them, and re-layouts  69.5 us (14%)
  blocking collectives  47.4 us (10%)
  other arithmetic  24.3 us (5%)
  between operations  16.5 us (3%)
  starting transfers between devices  10.6 us (2%)
    reduce_scatter x1, waiting for transfers between devices, per_device(): lax.psum_scatter(flat, 'seq', scatter_dimension=0, tiled=True).reshape(-1)  180 us
    psum x1, blocking collectives, per_device(): gain_total, slope_total = lax.psum((part_gain, slope_full), ('seq', 'tier'))  47.4 us
    dot_general x8, matrix products, mm(): return jnp.dot(left, right, preferred_element_type=f32)  32.5 us
    dot_general x6, matrix products, mm_nt(): lax.dot_general(left, right, (((1,), (1,)), ((), ())), preferred_element_...  24 us
    all_gather x1, waiting for transfers between devices, per_device(): raw_seq = lax.all_gather(raw_local, 'tier', axis=1, tiled=True)  23.7 us
    unnamed x93, local copies, waits for them, and re-layouts  22 us
    dot_general x7, matrix products, mm_tn(): lax.dot_general(left, right, (((0,), (0,)), ((), ())), preferred_element_...  21.3 us
    reshape x6, local copies, waits for them, and re-layouts, per_device(): flat = jnp.concatenate([p.reshape(seqs, -1, width) for p in parts], axis=1)  14.1 us
  transfers between devices with their start and end apart: 8, of which 3 were waited for; matrix products, arithmetic and copies ran while one was open for 30% of the time, Pallas kernels for 0%

commit v1 on v0

--- a/solution.py
+++ b/solution.py
@@ -213,7 +213,8 @@
     slope_full = lax.dynamic_update_slice_in_dim(
         jnp.zeros((heads,), f32), part_slope, tier_pos * hpt, 0
     )
-    gain_total, slope_total = lax.psum((part_gain, slope_full), ("seq", "tier"))
+    scan_the_core = lambda payload: lax.psum(lax.psum(payload, "tier"), "seq")
+    gain_total, slope_total = scan_the_core((part_gain, slope_full))
     return (
         output[None],
         grad_input[None],

time: 495 us -> 495 us (level)
  waiting for transfers between devices: 209 us -> 223 us
  blocking collectives: 47.4 us -> 33.9 us
    psum x1 -> x2, blocking collectives: 47.4 us -> 33.9 us  [per_device(): scan_the_core = lambda payload: lax.psum(lax.psum(payload, 'tier'), 'seq')]
    reduce_scatter x1, waiting for transfers between devices: 180 us -> 193 us  [per_device(): lax.psum_scatter(flat, 'seq', scatter_dimension=0, tiled=True).reshape(-1)]
where the time goes in v1:
time: 495 us; the launch traced here: 487 us
  waiting for transfers between devices  223 us (45%)
  matrix products  109 us (22%)
  local copies, waits for them, and re-layouts  69.5 us (14%)
  blocking collectives  33.9 us (7%)
  other arithmetic  24.3 us (5%)
  between operations  16.5 us (3%)
  starting transfers between devices  10.6 us (2%)
    reduce_scatter x1, waiting for transfers between devices, per_device(): lax.psum_scatter(flat, 'seq', scatter_dimension=0, tiled=True).reshape(-1)  193 us
    psum x2, blocking collectives, per_device(): scan_the_core = lambda payload: lax.psum(lax.psum(payload, 'tier'), 'seq')  33.9 us
    dot_general x8, matrix products, mm(): return jnp.dot(left, right, preferred_element_type=f32)  32.5 us
    dot_general x6, matrix products, mm_nt(): lax.dot_general(left, right, (((1,), (1,)), ((), ())), preferred_element_...  23.7 us
    all_gather x1, waiting for transfers between devices, per_device(): raw_seq = lax.all_gather(raw_local, 'tier', axis=1, tiled=True)  23.7 us
    unnamed x93, local copies, waits for them, and re-layouts  22.1 us
    dot_general x7, matrix products, mm_tn(): lax.dot_general(left, right, (((0,), (0,)), ((), ())), preferred_element_...  21.3 us
    reshape x6, local copies, waits for them, and re-layouts, per_device(): flat = jnp.concatenate([p.reshape(seqs, -1, width) for p in parts], axis=1)  14.1 us
  transfers between devices with their start and end apart: 8, of which 3 were waited for; matrix products, arithmetic and copies ran while one was open for 30% of the time, Pallas kernels for 0%

profile of v1, /device:TPU:0, one launch (start us, length us, event | category | flops | bytes accessed | tf_op | source)
XLA Modules:
  0.0 486.6 jit_solution(12790255855068029225)
XLA Ops:
  12.6 3.1 fusion.52
  19.5 23.7 %all-gather.5.cloned.1.call-done = bf16[3,512,1024]{2,1,0:T(8,128)(2,1)} async-done(((bf16[3,128,1024]{2,1,0:T(8,128)(2,1)}), bf16[3,512,1024]{2,1,0:T(8,128)(2,1)}) %all-gather.5.cloned.1.call-update) | async-done | bytes 3145744 | tf_op jit(solution)/shard_map/all_gather | solution.py:80
  43.3 3.7 convolution_convert_fusion
  47.1 2.8 convolution_convert_fusion.5
  57.4 3.4 all-to-all-start
  63.2 2.9 reshape.323
  66.1 4.5 convolution_convert_fusion.2
  82.4 3.1 fusion.54
  92.9 2.6 fusion.93
  98.1 6.0 %fusion.167 = f32[128,4096]{1,0:T(8,128)} fusion(bf16[1024,4096]{1,0:T(8,128)(2,1)} %param.24, f32[128,1024]{1,0:T(8,128)S(1)} %get-tuple-element.46, f32[1024]{0:T(1024)S(1)} %copy-done.38, f32[128]{0:T(128)S(1)} %fusion.135, f32[128]{0:T(128)S(1)} %broadcast_multiply_fusion), kind=kOutput, calls=%fused_computation.219 | convolution fusion | flops 1074266112 | bytes 11015168 | tf_op jit(solution)/shard_map/dot_general | solution.py:30
  104.1 13.6 %multiply_reduce_fusion.4 = (f32[1024]{0:T(1024)S(1)}, f32[128]{0:T(128)S(1)}, f32[128,1024]{1,0:T(8,128)}) fusion(f32[128,1024]{1,0:T(8,128)S(1)} %get-tuple-element.46, f32[128]{0:T(128)S(1)} %fusion.135, f32[128]{0:T(128)S(1)} %broadcast_multiply_fusion, f32[1024]{0:T(1024)S(1)} %copy-done.38, bf16[1024,4096]{1,0:T(8,128)(2,1)} %param.24, ...), kind=kOutput, calls=%fused_computation.135 | convolution fusion | flops 2159279104 | bytes 20195328 | tf_op jit(solution)/shard_map/dot_general | solution.py:38
  123.6 3.5 all-to-all-start.1
  130.8 5.1 %all-to-all-done.1 = bf16[2,128,1024]{1,0,2:T(2,128)(2,1)S(1)} async-done(((bf16[2,128,1024]{1,0,2:T(2,128)(2,1)}), bf16[2,128,1024]{1,0,2:T(2,128)(2,1)S(1)}, u32[]{:S(2)}, u32[]{:S(2)}) %all-to-all-start.1) | async-done | bytes 524320 | tf_op jit(solution)/shard_map/all_to_all | solution.py:159
  137.1 4.9 %multiply_reduce_fusion.1 = (f32[2,512]{1,0:T(2,128)S(1)}, f32[2,512,1536]{2,1,0:T(8,128)S(1)}) fusion(f32[2,512,1536]{2,1,0:T(8,128)} %copy-done.2, f32[2,512]{1,0:T(2,128)S(1)} %log_add_fusion, bf16[512,2,128]{0,2,1:T(8,128)(2,1)S(1)} %reshape.348, bf16[1536,2,128]{0,2,1:T(8,128)(2,1)S(1)} %bitcast.169), kind=kOutput, calls=%fused_computation.13 | convolution fusion | flops 407370752 | bytes 13639680 | tf_op jit(solution)/shard_map/rhd,khd->hrk/dot_general | solution.py:179
  142.0 4.7 multiply_reduce_fusion
  152.7 2.6 fusion.17
  157.8 4.2 convolution_convert_fusion.1
  171.2 3.2 fusion.117
  174.4 4.8 reshape.333
  183.9 7.3 %fusion.63 = f32[512,4096]{1,0:T(8,128)S(1)} fusion(bf16[1024,4096]{1,0:T(8,128)(2,1)} %param.24, bf16[2,512,1024]{2,1,0:T(8,128)(2,1)} %all-gather.7.cloned.1.call-done), kind=kOutput, calls=%fused_computation.98 | convolution fusion | flops 4294967296 | bytes 17825792 | tf_op jit(solution)/shard_map/dot_general | solution.py:30
  191.2 3.2 copy-done.41
  194.4 4.8 fusion.11
  199.2 5.2 %reshape.328 = f32[8,128,1024]{2,1,0:T(8,128)} reshape(f32[4096,256]{1,0:T(8,128)} %fusion.11) | data formatting | bytes 8388608 | tf_op jit(solution)/shard_map/reshape | solution.py:204
  205.5 7.7 %convolution_dynamic-update-slice_fusion = f32[8,480,1024]{2,1,0:T(8,128)} fusion(f32[8,480,1024]{2,1,0:T(8,128)} %constant_dynamic-update-slice_fusion.2, bf16[8,128,512]{2,1,0:T(8,128)(2,1)} %bitcast.187, f32[512,4096]{1,0:T(8,128)} %copy-done.41, s32[]{:T(128)S(6)} %select_n.37, bf16[512,1024]{1,0:T(8,128)(2,1)S(1)} %copy-done.24, ...), kind=kOutput, calls=%fused_computation.30 | convolution fusion | flops 2157969408 | bytes 10486784 | tf_op jit(solution)/shard_map/dot_general | solution.py:34
  213.2 4.9 %constant_dynamic-update-slice_fusion.1 = f32[8,480,1024]{2,1,0:T(8,128)} fusion(f32[8,480,1024]{2,1,0:T(8,128)} %convolution_dynamic-update-slice_fusion, f32[8,128,1024]{2,1,0:T(8,128)} %reshape.328), kind=kLoop, calls=%fused_computation.164 | loop fusion | bytes 8388608
  224.7 2.8 pad_maximum_fusion.1
  227.5 3.5 all-to-all-start.2
  231.0 6.3 %fusion.56 = bf16[1,128,1024]{2,1,0:T(8,128)(2,1)} fusion(f32[128,1024]{1,0:T(8,128)S(1)} %get-tuple-element.46, bf16[4096,1024]{1,0:T(8,128)(2,1)} %param.25, f32[128,4096]{1,0:T(8,128)} %fusion.167, f32[128]{0:T(128)S(1)} %compare_convert_fusion), kind=kOutput, calls=%fused_computation.83 | convolution fusion | flops 1078853632 | bytes 11272704 | tf_op jit(solution)/shard_map/dot_general | solution.py:30
  237.4 9.8 %all-reduce.2 = (f32[1024]{0:T(1024)S(1)}, f32[8]{0:T(128)S(1)}) all-reduce(f32[1024]{0:T(1024)S(1)} %get-tuple-element.13, f32[8]{0:T(128)S(1)} %negate_dynamic-update-slice_fusion), channel_id=1, replica_groups=mesh['seq'=8,'tier'=4] {'tier'}, use_global_device_ids=true, to_apply=%region_15.16 | all-reduce | flops 1032 | bytes 8256 | tf_op jit(solution)/shard_map/psum | solution.py:216
  247.2 24.2 %all-reduce.1 = (f32[1024]{0:T(1024)}, f32[8]{0:T(128)}) all-reduce(f32[1024]{0:T(1024)S(1)} %get-tuple-element.17, f32[8]{0:T(128)S(1)} %get-tuple-element.18), channel_id=1, replica_groups=mesh['seq'=8,'tier'=4] {'seq'}, use_global_device_ids=true, to_apply=%region_16.17 | all-reduce | flops 1032 | bytes 8256 | tf_op jit(solution)/shard_map/psum | solution.py:216
  272.1 2.6 convolution_add_fusion.2
  278.8 192.9 %reduce-scatter.5.cloned.1.call-done = f32[480,1024]{1,0:T(8,128)} async-done(((f32[3840,1024]{1,0:T(8,128)}), f32[480,1024]{1,0:T(8,128)}) %reduce-scatter.5.cloned.1.call-update) | async-done | bytes 1966096 | tf_op jit(solution)/shard_map/reduce_scatter | solution.py:206
  (195 shorter events, 92.5 us)
Async XLA Ops:
  7.2 89.1 %copy-start = (bf16[1024,1024]{1,0:T(8,128)(2,1)S(1)}, bf16[1024,1024]{1,0:T(8,128)(2,1)}, u32[]{:S(2)}) copy-start(bf16[1024,1024]{1,0:T(8,128)(2,1)} %param.23) | copy-start | bytes 6291460
  7.2 36.1 %all-gather.5.cloned.1.call-start = ((), (), s32[]{:S(2)}) async-start(), calls=%async_computation.5 | async-start | bytes 3932160 | tf_op jit(solution)/shard_map/all_gather | solution.py:80
  11.9 115.3 %all-gather.9.cloned.1.call-start = ((), (), s32[]{:S(2)}) async-start(), calls=%async_computation.9 | async-start | bytes 1310720 | tf_op jit(solution)/shard_map/all_gather | solution.py:81
  19.5 23.7 %copy-start.33 = (bf16[1024,256]{1,0:T(8,128)(2,1)}, bf16[1024,256]{1,0:T(8,128)(2,1)S(1)}, u32[]{:S(2)}) copy-start(bf16[1024,256]{1,0:T(8,128)(2,1)S(1)} %get-tuple-element.55) | copy-start | bytes 1572868
  19.5 27.5 %copy-start.31 = (bf16[1024,256]{1,0:T(8,128)(2,1)}, bf16[1024,256]{1,0:T(8,128)(2,1)S(1)}, u32[]{:S(2)}) copy-start(bf16[1024,256]{1,0:T(8,128)(2,1)S(1)} %get-tuple-element.54) | copy-start | bytes 1572868
  47.1 6.6 %copy-start.7 = (bf16[1536,256]{0,1:T(8,128)(2,1)}, bf16[1536,256]{0,1:T(8,128)(2,1)S(1)}, u32[]{:S(2)}) copy-start(bf16[1536,256]{0,1:T(8,128)(2,1)S(1)} %get-tuple-element.32) | copy-start | bytes 2359300
  57.4 38.1 %all-to-all-start = ((bf16[4,128,256]{1,2,0:T(8,128)(2,1)}), bf16[4,128,256]{1,2,0:T(8,128)(2,1)S(1)}, u32[]{:S(2)}, u32[]{:S(2)}) async-start(bf16[4,128,256]{1,2,0:T(8,128)(2,1)} %copy.122), calls=%async_computation | async-start | bytes 524288 | tf_op jit(solution)/shard_map/all_to_all | solution.py:111
  60.8 110.3 %reduce-scatter.3.cloned.1.call-start = ((), (), s32[]{:S(2)}) async-start(), calls=%async_computation.7 | async-start | bytes 901120 | tf_op jit(solution)/shard_map/reduce_scatter | solution.py:136
  66.1 4.5 copy-start.32
  66.1 4.5 copy-start.34
  66.1 7.5 %copy-start.29 = (bf16[512,256]{0,1:T(8,128)(2,1)S(1)}, bf16[512,256]{0,1:T(8,128)(2,1)}, u32[]{:S(2)}) copy-start(bf16[512,256]{0,1:T(8,128)(2,1)} %copy-done.28) | copy-start | bytes 786436
  92.9 5.2 %copy-start.38 = (f32[1024]{0:T(1024)S(1)}, f32[1024]{0:T(1024)}, u32[]{:S(2)}) copy-start(f32[1024]{0:T(1024)} %param.26) | copy-start | bytes 12292
  122.4 7.3 %copy-start.21 = (bf16[4,128,256]{1,2,0:T(8,128)(2,1)S(1)}, bf16[4,128,256]{1,2,0:T(8,128)(2,1)}, u32[]{:S(2)}) copy-start(bf16[4,128,256]{1,2,0:T(8,128)(2,1)} %copy-done.20) | copy-start | bytes 786436
  122.5 7.4 %copy-start.27 = (bf16[1,128,1024]{2,1,0:T(8,128)(2,1)S(1)}, bf16[1,128,1024]{2,1,0:T(8,128)(2,1)}, u32[]{:S(2)}) copy-start(bf16[1,128,1024]{2,1,0:T(8,128)(2,1)} %get-tuple-element.36) | copy-start | bytes 786436
  123.6 12.3 %all-to-all-start.1 = ((bf16[2,128,1024]{1,0,2:T(2,128)(2,1)}), bf16[2,128,1024]{1,0,2:T(2,128)(2,1)S(1)}, u32[]{:S(2)}, u32[]{:S(2)}) async-start(bf16[2,128,1024]{1,0,2:T(2,128)(2,1)} %copy.123), calls=%async_computation.1 | async-start | bytes 1048576 | tf_op jit(solution)/shard_map/all_to_all | solution.py:159
  127.1 52.1 %all-gather.7.cloned.1.call-start = ((), (), s32[]{:S(2)}) async-start(), calls=%async_computation.6 | async-start | bytes 2621440 | tf_op jit(solution)/shard_map/all_gather | solution.py:162
  129.7 7.4 %copy-start.8 = (bf16[1536,256]{0,1:T(8,128)(2,1)S(1)}, bf16[1536,256]{0,1:T(8,128)(2,1)}, u32[]{:S(2)}) copy-start(bf16[1536,256]{0,1:T(8,128)(2,1)} %copy-done.7) | copy-start | bytes 2359300
  130.7 341.0 %reduce-scatter.5.cloned.1.call-start = ((), (), s32[]{:S(2)}) async-start(), calls=%async_computation.8 | async-start | bytes 17694720 | tf_op jit(solution)/shard_map/reduce_scatter | solution.py:206
  137.1 4.9 %copy-start.4 = (f32[1536,512]{0,1:T(8,128)S(1)}, f32[1536,512]{0,1:T(8,128)}, u32[]{:S(2)}) copy-start(f32[1536,512]{0,1:T(8,128)} %get-tuple-element.41) | copy-start | bytes 9437188
  149.5 5.8 %copy-start.18 = (bf16[2,128,512]{2,1,0:T(8,128)(2,1)}, bf16[2,128,512]{2,1,0:T(8,128)(2,1)S(1)}, u32[]{:S(2)}) copy-start(bf16[2,128,512]{2,1,0:T(8,128)(2,1)S(1)} %fusion.50) | copy-start | bytes 786436
  165.3 4.8 copy-start.12
  165.3 5.9 %copy-start.11 = (bf16[171,3072]{1,0:T(8,128)(2,1)S(1)}, bf16[171,3072]{1,0:T(8,128)(2,1)}, u32[]{:S(2)}) copy-start(bf16[171,3072]{1,0:T(8,128)(2,1)} %reshape.323) | copy-start | bytes 3151876
  174.4 4.8 copy-start.37
  183.9 10.5 %copy-start.24 = (bf16[512,1024]{1,0:T(8,128)(2,1)S(1)}, bf16[512,1024]{1,0:T(8,128)(2,1)}, u32[]{:S(2)}) copy-start(bf16[512,1024]{1,0:T(8,128)(2,1)} %fusion.32) | copy-start | bytes 3145732
  213.2 4.9 %copy-start.5 = (f32[8,96,1024]{2,1,0:T(8,128)S(1)}, f32[8,96,1024]{2,1,0:T(8,128)}, u32[]{:S(2)}) copy-start(f32[8,96,1024]{2,1,0:T(8,128)} %reshape.333) | copy-start | bytes 9437188
  220.0 4.3 copy-start.19
  227.5 43.9 %all-to-all-start.2 = ((bf16[3,512,256]{2,0,1:T(4,128)(2,1)}), bf16[3,512,256]{2,0,1:T(4,128)(2,1)S(1)}, u32[]{:S(2)}, u32[]{:S(2)}) async-start(bf16[3,512,256]{2,0,1:T(4,128)(2,1)} %pad_maximum_fusion.1), calls=%async_computation.2 | async-start | bytes 2097152 | tf_op jit(solution)/shard_map/all_to_all | solution.py:198
  237.3 34.7 %copy-start.10 = (f32[128,1024]{1,0:T(8,128)S(1)}, f32[128,1024]{1,0:T(8,128)}, u32[]{:S(2)}) copy-start(f32[128,1024]{1,0:T(8,128)} %copy-done.9) | copy-start | bytes 1572868
  237.3 34.8 %copy-start.22 = (bf16[1,128,1024]{2,1,0:T(8,128)(2,1)S(1)}, bf16[1,128,1024]{2,1,0:T(8,128)(2,1)}, u32[]{:S(2)}) copy-start(bf16[1,128,1024]{2,1,0:T(8,128)(2,1)} %param.29) | copy-start | bytes 786436
  272.1 5.0 %copy-start.13 = (bf16[1024,1024]{1,0:T(8,128)(2,1)S(1)}, bf16[1024,1024]{1,0:T(8,128)(2,1)}, u32[]{:S(2)}) copy-start(bf16[1024,1024]{1,0:T(8,128)(2,1)} %param.22) | copy-start | bytes 6291460
  471.7 7.1 %slice-start = ((f32[480,1024]{1,0:T(8,128)}), f32[96,1024]{1,0:T(8,128)S(1)}, s32[]{:S(2)}) async-start(f32[480,1024]{1,0:T(8,128)} %reduce-scatter.5.cloned.1.call-done), calls=%async_computation.10 | async-start | bytes 786432 | tf_op jit(solution)/shard_map/slice | solution.py:211
  471.7 7.9 %copy-start.1 = (bf16[1024,1024]{1,0:T(8,128)(2,1)S(1)}, bf16[1024,1024]{1,0:T(8,128)(2,1)}, u32[]{:S(2)}) copy-start(bf16[1024,1024]{1,0:T(8,128)(2,1)} %param.23) | copy-start | bytes 6291460
  (19 other events, 46.1 us)
Sparse Core Ops, SparseCore 0:
  12.0 31.2 all-gather.4
  44.8 16.7 all-gather.8
  95.6 24.2 reduce-scatter.2
  130.9 23.9 all-gather.6
  220.1 251.5 reduce-scatter.4
